TPU v7x, 128 devices: a whole 4x4x4 slice. The times are simulated.
128 devices in a mesh: dp: 64 (over z, y_lo, x, core), mp: 2 (over y_hi).
Axes of the slice: x: 4, y: 4 (y_hi: 2, y_lo: 2; y = y_hi * 2 + y_lo), z: 4, core: 2. Of those that a mesh axis runs over, the one named last changes fastest.
Arguments:
- images: bfloat16 [128, 197, 384], P('dp'), may hold values from -6 to 6
- routes: int32 [1, 128, 197, 2], P(None, 'dp'), may hold values from 0 to 3, all different within a row; in each aligned block of 197 rows (0 to 196, 197 to 393, ..., all dimensions but the last counted through in order) at most 104 rows name the same one
- w_qkv: bfloat16 [1, 384, 3, 384], P(None, 'dp', None, 'mp'), may hold values from -0.3125 to 0.3125
- w_proj: bfloat16 [1, 384, 384], P(None, 'mp', 'dp'), may hold values from -2 to 2
- w_in: bfloat16 [1, 4, 384, 1536], P(None, None, 'dp', 'mp'), may hold values from -0.3125 to 0.3125
- w_out: bfloat16 [1, 4, 1536, 384], P(None, None, 'mp', 'dp'), may hold values from -0.3125 to 0.3125
- w_router: bfloat16 [1, 384, 4], P(None, 'dp'), may hold values from -0.625 to 0.625
- ln_gain: bfloat16 [1, 2, 384], P(None, None, 'dp'), may hold values from 0.5 to 1.5
- ln_bias: bfloat16 [1, 2, 384], P(None, None, 'dp'), may hold values from -3 to 3
- cotangent: bfloat16 [128, 197, 384], P('dp'), may hold values from -6 to 6
Outputs:
- activations: float32 [128, 197, 384], P('dp')
- grad_images: float32 [128, 197, 384], P('dp')
- grad_qkv: float32 [1, 384, 3, 384], P(None, 'dp', None, 'mp')
- grad_proj: float32 [1, 384, 384], P(None, 'mp', 'dp')
- grad_in: float32 [1, 4, 384, 1536], P(None, None, 'dp', 'mp')
- grad_out: float32 [1, 4, 1536, 384], P(None, None, 'mp', 'dp')
- grad_router: float32 [1, 384, 4], P(None, 'dp')
- grad_gain: float32 [1, 2, 384], P(None, None, 'dp')
- grad_bias: float32 [1, 2, 384], P(None, None, 'dp')
Inputs may be any that keep to these rules, and one draw needn't show every extreme that they name: `routes`: in each block, each aligned group of 1 images names every expert in at most 104 of its tokens, and some group names some expert in exactly 104; a token's two experts differ.
All inputs are finite; a program needn't handle non-finite values.
Results may differ from a plain program's by a relative error of at most 0.024.
Values may be sent and summed in bfloat16 or wider, within the bound.
A program may use at most 128 MiB of HBM per device.

v0:
```python
import jax
import jax.numpy as jnp
from jax import lax
from jax.sharding import PartitionSpec as P

HD = 64
EXPERTS = 4
TOPK = 2
LAYERS = 1
MICRO = 2
IMG_MB = 1
CAP = 104
EPSILON = 1e-06


def norm_forward(field, gain_row, shift_row):
    mean_value = jnp.mean(field, axis=-1, keepdims=True)
    centered = field - mean_value
    inverse = lax.rsqrt(jnp.mean(centered * centered, axis=-1, keepdims=True) + EPSILON)
    normed = centered * inverse
    return (normed * gain_row + shift_row, normed, inverse)


def norm_backward(grad_out, normed, inverse, gain_row):
    grad_gain = jnp.sum(grad_out * normed, axis=0)
    grad_shift = jnp.sum(grad_out, axis=0)
    scaled = grad_out * gain_row
    grad_in = inverse * (
        scaled
        - jnp.mean(scaled, axis=-1, keepdims=True)
        - normed * jnp.mean(scaled * normed, axis=-1, keepdims=True)
    )
    return (grad_in, grad_gain, grad_shift)


def slot_positions(chosen_ids):
    labels = jnp.arange(EXPERTS, dtype=jnp.int32)
    hit_counts = jnp.sum((chosen_ids[:, :, None] == labels).astype(jnp.int32), axis=1)
    before = jnp.cumsum(hit_counts, axis=0) - hit_counts
    return jnp.take_along_axis(before, chosen_ids, axis=1)


def gelu_slope(inner_pre):
    cumulative = 0.5 * (1.0 + jax.scipy.special.erf(inner_pre * 0.7071067811865476))
    density = jnp.exp(-0.5 * inner_pre * inner_pre) * 0.3989422804014327
    return cumulative + inner_pre * density


def fetch_layer(layer_index, w_qkv, w_proj, w_in, w_out, w_router, ln_gain, ln_bias):
    return (
        lax.all_gather(w_qkv[layer_index], "dp", axis=0, tiled=True),
        lax.all_gather(w_proj[layer_index], "dp", axis=1, tiled=True),
        lax.all_gather(w_in[layer_index], "dp", axis=1, tiled=True),
        lax.all_gather(w_out[layer_index], "dp", axis=2, tiled=True),
        lax.all_gather(w_router[layer_index], "dp", axis=0, tiled=True),
        lax.all_gather(ln_gain[layer_index], "dp", axis=1, tiled=True),
        lax.all_gather(ln_bias[layer_index], "dp", axis=1, tiled=True),
    )


def layer_forward(field, chosen_ids, weights):
    w_qkv, w_proj, w_in, w_out, w_router, ln_gain, ln_bias = weights
    image_count, length, model_width = field.shape
    row_count = image_count * length
    head_count = w_qkv.shape[2] // HD
    score_scale = HD ** (-0.5)
    gain_rows = ln_gain.astype(jnp.float32)
    shift_rows = ln_bias.astype(jnp.float32)
    flat = field.reshape(row_count, model_width)
    first, normed_one, inverse_one = norm_forward(flat, gain_rows[0], shift_rows[0])
    first = first.astype(jnp.bfloat16)
    projected = jnp.einsum("rd,dcf->rcf", first, w_qkv, preferred_element_type=jnp.float32).astype(
        jnp.bfloat16
    )
    projected = projected.reshape(image_count, length, 3, head_count, HD)
    queries = projected[:, :, 0]
    key_rows = projected[:, :, 1]
    value_rows = projected[:, :, 2]
    scores = (
        jnp.einsum("bqhe,bkhe->bhqk", queries, key_rows, preferred_element_type=jnp.float32)
        * score_scale
    )
    log_total = jax.nn.logsumexp(scores, axis=-1)
    attn_weights = jnp.exp(scores - log_total[..., None]).astype(jnp.bfloat16)
    attended = jnp.einsum(
        "bhqk,bkhe->bqhe", attn_weights, value_rows, preferred_element_type=jnp.float32
    )
    attended = attended.astype(jnp.bfloat16).reshape(row_count, head_count * HD)
    partial_attn = jnp.dot(attended, w_proj, preferred_element_type=jnp.float32)
    hidden = flat + lax.psum(partial_attn, "mp")
    second, normed_two, inverse_two = norm_forward(hidden, gain_rows[1], shift_rows[1])
    second = second.astype(jnp.bfloat16)
    logits = jnp.dot(second, w_router, preferred_element_type=jnp.float32)
    router = jax.nn.softmax(logits, axis=-1)
    labels = jnp.arange(EXPERTS, dtype=jnp.int32)
    chosen = (chosen_ids[:, :, None] == labels).astype(jnp.float32)
    gate_values = jnp.sum(router[:, None, :] * chosen, axis=-1)
    slot_index = (chosen_ids * CAP + slot_positions(chosen_ids)).reshape(-1)
    owners = (
        jnp.full((EXPERTS * CAP,), row_count, jnp.int32)
        .at[slot_index]
        .set(jnp.repeat(jnp.arange(row_count, dtype=jnp.int32), TOPK))
    )
    slot_gate = jnp.zeros((EXPERTS * CAP,), jnp.float32).at[slot_index].set(gate_values.reshape(-1))
    padded = jnp.concatenate([second, jnp.zeros((1, model_width), jnp.bfloat16)], axis=0)
    slot_rows = jnp.take(padded, owners, axis=0).reshape(EXPERTS, CAP, model_width)
    inner_pre = jnp.einsum("ecd,edf->ecf", slot_rows, w_in, preferred_element_type=jnp.float32)
    activated = jax.nn.gelu(inner_pre, approximate=False).astype(jnp.bfloat16)
    produced = jnp.einsum("ecf,efd->ecd", activated, w_out, preferred_element_type=jnp.float32)
    produced = produced.reshape(EXPERTS * CAP, model_width)
    picked = jnp.take(produced, slot_index, axis=0).reshape(row_count, TOPK, model_width)
    partial_moe = jnp.sum(gate_values[:, :, None] * picked, axis=1)
    output = hidden + lax.psum(partial_moe.astype(jnp.bfloat16), "mp").astype(jnp.float32)
    record = (
        normed_one,
        inverse_one,
        first,
        projected,
        log_total,
        attended,
        normed_two,
        inverse_two,
        second,
        router,
        chosen,
        slot_index,
        owners,
        slot_gate,
        slot_rows,
        inner_pre,
        activated,
        picked,
    )
    return (output.reshape(image_count, length, model_width), record)


def layer_backward(grad_field, record, weights):
    w_qkv, w_proj, w_in, w_out, w_router, ln_gain, ln_bias = weights
    (
        normed_one,
        inverse_one,
        first,
        projected,
        log_total,
        attended,
        normed_two,
        inverse_two,
        second,
        router,
        chosen,
        slot_index,
        owners,
        slot_gate,
        slot_rows,
        inner_pre,
        activated,
        picked,
    ) = record
    image_count, length, model_width = grad_field.shape
    row_count = image_count * length
    head_count = projected.shape[3]
    score_scale = HD ** (-0.5)
    gain_rows = ln_gain.astype(jnp.float32)
    grad_flat = grad_field.reshape(row_count, model_width)
    padded_grad = jnp.concatenate([grad_flat, jnp.zeros((1, model_width), jnp.float32)], axis=0)
    grad_slots = (jnp.take(padded_grad, owners, axis=0) * slot_gate[:, None]).astype(jnp.bfloat16)
    grad_slots = grad_slots.reshape(EXPERTS, CAP, model_width)
    grad_w_out = jnp.einsum(
        "ecf,ecd->efd", activated, grad_slots, preferred_element_type=jnp.float32
    )
    grad_act = jnp.einsum("ecd,efd->ecf", grad_slots, w_out, preferred_element_type=jnp.float32)
    grad_inner = (grad_act * gelu_slope(inner_pre)).astype(jnp.bfloat16)
    grad_w_in = jnp.einsum(
        "ecd,ecf->edf", slot_rows, grad_inner, preferred_element_type=jnp.float32
    )
    grad_slot_rows = jnp.einsum(
        "ecf,edf->ecd", grad_inner, w_in, preferred_element_type=jnp.float32
    )
    grad_slot_rows = grad_slot_rows.reshape(EXPERTS * CAP, model_width)
    partial_second = jnp.sum(
        jnp.take(grad_slot_rows, slot_index, axis=0).reshape(row_count, TOPK, model_width), axis=1
    )
    partial_gate = jnp.sum(picked * grad_flat[:, None, :], axis=-1)
    grad_second, grad_gate = lax.psum((partial_second, partial_gate), "mp")
    grad_router = jnp.sum(grad_gate[:, :, None] * chosen, axis=1)
    grad_logits = router * (grad_router - jnp.sum(router * grad_router, axis=-1, keepdims=True))
    grad_logits = grad_logits.astype(jnp.bfloat16)
    grad_w_router = jnp.dot(second.T, grad_logits, preferred_element_type=jnp.float32)
    grad_second = grad_second + jnp.dot(grad_logits, w_router.T, preferred_element_type=jnp.float32)
    grad_from_norm, grad_gain_two, grad_shift_two = norm_backward(
        grad_second, normed_two, inverse_two, gain_rows[1]
    )
    grad_hidden = grad_flat + grad_from_norm
    grad_hidden_low = grad_hidden.astype(jnp.bfloat16)
    grad_w_proj = jnp.dot(attended.T, grad_hidden_low, preferred_element_type=jnp.float32)
    grad_attended = jnp.dot(grad_hidden_low, w_proj.T, preferred_element_type=jnp.float32).astype(
        jnp.bfloat16
    )
    grad_attended = grad_attended.reshape(image_count, length, head_count, HD)
    queries = projected[:, :, 0]
    key_rows = projected[:, :, 1]
    value_rows = projected[:, :, 2]
    scores = (
        jnp.einsum("bqhe,bkhe->bhqk", queries, key_rows, preferred_element_type=jnp.float32)
        * score_scale
    )
    probs = jnp.exp(scores - log_total[..., None])
    grad_values = jnp.einsum(
        "bhqk,bqhe->bkhe",
        probs.astype(jnp.bfloat16),
        grad_attended,
        preferred_element_type=jnp.float32,
    )
    grad_probs = jnp.einsum(
        "bqhe,bkhe->bhqk", grad_attended, value_rows, preferred_element_type=jnp.float32
    )
    grad_scores = (
        probs * (grad_probs - jnp.sum(probs * grad_probs, axis=-1, keepdims=True))
    ).astype(jnp.bfloat16)
    grad_queries = (
        jnp.einsum("bhqk,bkhe->bqhe", grad_scores, key_rows, preferred_element_type=jnp.float32)
        * score_scale
    )
    grad_keys = (
        jnp.einsum("bhqk,bqhe->bkhe", grad_scores, queries, preferred_element_type=jnp.float32)
        * score_scale
    )
    grad_projected = jnp.stack([grad_queries, grad_keys, grad_values], axis=2).astype(jnp.bfloat16)
    grad_projected = grad_projected.reshape(row_count, 3, head_count * HD)
    grad_w_qkv = jnp.einsum(
        "rd,rcf->dcf", first, grad_projected, preferred_element_type=jnp.float32
    )
    partial_first = jnp.einsum(
        "rcf,dcf->rd", grad_projected, w_qkv, preferred_element_type=jnp.float32
    )
    grad_first = lax.psum(partial_first.astype(jnp.bfloat16), "mp").astype(jnp.float32)
    grad_input_norm, grad_gain_one, grad_shift_one = norm_backward(
        grad_first, normed_one, inverse_one, gain_rows[0]
    )
    grad_input = grad_hidden + grad_input_norm
    grads = (
        grad_w_qkv,
        grad_w_proj,
        grad_w_in,
        grad_w_out,
        grad_w_router,
        jnp.stack([grad_gain_one, grad_gain_two]),
        jnp.stack([grad_shift_one, grad_shift_two]),
    )
    return (grad_input.reshape(image_count, length, model_width), grads)


def local(images, routes, w_qkv, w_proj, w_in, w_out, w_router, ln_gain, ln_bias, cotangent):
    outputs = []
    grad_parts = []
    totals = []
    for micro_index in range(MICRO):
        start_row = micro_index * IMG_MB
        field = images[start_row : start_row + IMG_MB].astype(jnp.float32)
        fetched = []
        layer_index = 0
        weights = fetch_layer(layer_index, w_qkv, w_proj, w_in, w_out, w_router, ln_gain, ln_bias)
        layer_routes = routes[layer_index, start_row : start_row + IMG_MB].reshape(-1, TOPK)
        field, record = layer_forward(field, layer_routes, weights)
        records = [record]
        fetched.append(weights)
        outputs.append(field)
        grad_field = cotangent[start_row : start_row + IMG_MB].astype(jnp.float32)
        layer_grads = [None] * LAYERS
        for layer_index in reversed(range(LAYERS)):
            weights = fetch_layer(
                layer_index, w_qkv, w_proj, w_in, w_out, w_router, ln_gain, ln_bias
            )
            grad_field, grads = layer_backward(grad_field, records[layer_index], weights)
            layer_grads[layer_index] = grads
        grad_parts.append(grad_field)
        if micro_index == 0:
            totals = layer_grads
        else:
            totals = [
                jax.tree.map(jnp.add, earlier, later) for earlier, later in zip(totals, layer_grads)
            ]
    layer_index = 0
    held = totals[layer_index]
    shards = [
        (
            lax.psum_scatter(held[0], "dp", scatter_dimension=0, tiled=True),
            lax.psum_scatter(held[1], "dp", scatter_dimension=1, tiled=True),
            lax.psum_scatter(held[2], "dp", scatter_dimension=1, tiled=True),
            lax.psum_scatter(held[3], "dp", scatter_dimension=2, tiled=True),
            lax.psum_scatter(held[4], "dp", scatter_dimension=0, tiled=True),
            lax.psum_scatter(held[5], "dp", scatter_dimension=1, tiled=True),
            lax.psum_scatter(held[6], "dp", scatter_dimension=1, tiled=True),
        )
    ]
    return (
        jnp.concatenate(outputs, axis=0),
        jnp.concatenate(grad_parts, axis=0),
        jnp.stack([piece[0] for piece in shards]),
        jnp.stack([piece[1] for piece in shards]),
        jnp.stack([piece[2] for piece in shards]),
        jnp.stack([piece[3] for piece in shards]),
        jnp.stack([piece[4] for piece in shards]),
        jnp.stack([piece[5] for piece in shards]),
        jnp.stack([piece[6] for piece in shards]),
    )


def solution(mesh):
    in_specs = (
        P("dp", None, None),
        P(None, "dp", None, None),
        P(None, "dp", None, "mp"),
        P(None, "mp", "dp"),
        P(None, None, "dp", "mp"),
        P(None, None, "mp", "dp"),
        P(None, "dp", None),
        P(None, None, "dp"),
        P(None, None, "dp"),
        P("dp", None, None),
    )
    out_specs = (
        P("dp", None, None),
        P("dp", None, None),
        P(None, "dp", None, "mp"),
        P(None, "mp", "dp"),
        P(None, None, "dp", "mp"),
        P(None, None, "mp", "dp"),
        P(None, "dp", None),
        P(None, None, "dp"),
        P(None, None, "dp"),
    )
    return jax.shard_map(local, mesh=mesh, in_specs=in_specs, out_specs=out_specs, check_vma=False)
```

profile of v0, /device:TPU:0, one launch (start us, length us, event | category | flops | bytes accessed | tf_op | source)
XLA Modules:
  0.0 1335.0 jit_solution(13719838613397084062)
XLA Ops:
  10.3 83.9 %all-gather.1 = bf16[1,2,384]{1,0,2:T(2,128)(2,1)S(1)} all-gather(bf16[1,2,6]{1,0,2:T(2,128)(2,1)S(1)} %copy.153), channel_id=3, replica_groups=mesh['dp'=64,'mp'=2] {'dp'}, dimensions={2}, use_global_device_ids=true | all-gather | bytes 1560 | tf_op jit(solution)/shard_map/all_gather | solution.py:57
  96.1 77.0 %all-gather = bf16[1,2,384]{1,0,2:T(2,128)(2,1)S(1)} all-gather(bf16[1,2,6]{1,0,2:T(2,128)(2,1)S(1)} %copy.152), channel_id=2, replica_groups=mesh['dp'=64,'mp'=2] {'dp'}, dimensions={2}, use_global_device_ids=true | all-gather | bytes 1560 | tf_op jit(solution)/shard_map/all_gather | solution.py:56
  175.1 78.9 %all-gather.3 = bf16[1,192,384]{1,0,2:T(2,128)(2,1)S(1)} all-gather(bf16[1,192,6]{1,0,2:T(2,128)(2,1)S(1)} %copy.157), channel_id=5, replica_groups=mesh['dp'=64,'mp'=2] {'dp'}, dimensions={2}, use_global_device_ids=true | all-gather | bytes 149760 | tf_op jit(solution)/shard_map/all_gather | solution.py:52
  255.8 78.6 %all-gather.2 = bf16[1,384,3,192]{3,2,0,1:T(4,128)(2,1)S(1)} all-gather(bf16[1,6,3,192]{3,2,0,1:T(4,128)(2,1)S(1)} %bitcast.432), channel_id=4, replica_groups=mesh['dp'=64,'mp'=2] {'dp'}, dimensions={1}, use_global_device_ids=true | all-gather | bytes 449280 | tf_op jit(solution)/shard_map/all_gather | solution.py:51
  343.7 5.9 gather_fusion.3
  353.3 5.9 gather_fusion
  368.4 78.4 %all-gather.4 = bf16[1,384,4]{2,0,1:T(2,128)(2,1)S(1)} all-gather(bf16[1,6,4]{2,0,1:T(2,128)(2,1)S(1)} %copy.161), channel_id=6, replica_groups=mesh['dp'=64,'mp'=2] {'dp'}, dimensions={1}, use_global_device_ids=true | all-gather | bytes 3120 | tf_op jit(solution)/shard_map/all_gather | solution.py:55
  470.5 85.3 %all-gather.12.cloned.1.call-done = bf16[1,4,768,384]{2,1,0,3:T(4,128)(2,1)} async-done(((bf16[1,4,768,6]{2,1,0,3:T(4,128)(2,1)}), bf16[1,4,768,384]{2,1,0,3:T(4,128)(2,1)}) %all-gather.12.cloned.1.call-update) | async-done | bytes 2359312 | tf_op jit(solution)/shard_map/all_gather | solution.py:54
  555.9 5.4 copy.169
  581.0 15.0 %all-reduce.16 = (f32[197,2]{1,0:T(8,128)}, f32[197,2]{1,0:T(8,128)}) all-reduce(f32[197,2]{1,0:T(8,128)} %reduce_sum.430, f32[197,2]{1,0:T(8,128)S(1)} %reduce_sum.420), channel_id=1, replica_groups=mesh['dp'=64,'mp'=2] {'mp'}, use_global_device_ids=true, to_apply=%region_49.54 | all-reduce | flops 788 | bytes 6304 | tf_op jit(solution)/shard_map/psum | solution.py:184
  599.8 3.6 scatter_custom_fusion.2
  604.2 4.1 fusion.30
  625.0 4.1 fusion.27
  632.9 4.1 fusion.175
  655.4 5.7 convolution_add_fusion.1
  661.0 30.0 %all-reduce.27.cloned.1.call-done = (f32[197,384]{1,0:T(8,128)}, f32[197,384]{1,0:T(8,128)}) async-done(((f32[197,384]{1,0:T(8,128)}, f32[197,384]{1,0:T(8,128)}), (f32[197,384]{1,0:T(8,128)}, f32[197,384]{1,0:T(8,128)})) %all-reduce.27.cloned.1.call-update) | async-done | bytes 605200 | tf_op jit(solution)/shard_map/psum | solution.py:184
  704.9 7.5 copy.189
  712.4 5.2 copy.190
  721.7 145.4 %fusion = f32[192,8]{0,1:T(8,128)S(1)} fusion(f32[192,384]{0,1:T(8,128)S(1)} %convolution_add_fusion.3), kind=kCustom, calls=%all-reduce-scatter | all-reduce-scatter fusion | flops 98305 | bytes 301568
  876.8 9.5 collective-permute-start.9
  891.0 3.8 collective-permute-start.6
  899.4 4.3 collective-permute-start.3
  918.6 276.1 %all-reduce.14 = (f32[384,4]{0,1:T(4,128)S(1)}, f32[2,384]{1,0:T(2,128)S(1)}, f32[2,384]{1,0:T(2,128)S(1)}) all-reduce(f32[384,4]{0,1:T(4,128)S(1)} %convolution_add_fusion.6, f32[2,384]{1,0:T(2,128)S(1)} %maximum_add_fusion, f32[2,384]{1,0:T(2,128)S(1)} %maximum_add_fusion.1), channel_id=13, replica_groups=mesh['dp'=64,'mp'=2] {'dp'}, use_global_device_ids=true, to_apply=%region_62.67.clone | all-reduce | flops 3072 | bytes 24576
  1196.6 126.3 %all-reduce.25.cloned.1.call-done = (f32[384,3,192]{2,0,1:T(8,128)}, f32[4,384,768]{2,0,1:T(4,128)}, f32[4,768,384]{1,0,2:T(4,128)}) async-done(((f32[384,3,192]{2,0,1:T(8,128)}, f32[4,384,768]{2,0,1:T(4,128)}, f32[4,768,384]{1,0,2:T(4,128)}), (f32[384,3,192]{2,0,1:T(8,128)}, f32[4,384,768]{2,0,1:T(4,128)}, f32[4,768,384]{1,0,2:T(4,128)})) %all-reduce.25.cloned.1.call-update) | async-done | bytes 10321936
  (484 shorter events, 171.9 us)
Async XLA Ops:
  8.0 446.8 %all-reduce.29.cloned.1.call-start = ((), (), s32[]{:S(2)}) async-start(), calls=%async_computation.4 | async-start | bytes 1228800 | tf_op jit(solution)/shard_map/psum | solution.py:90
  96.1 239.6 %copy-start.52 = (f32[384]{0:T(512)}, f32[384]{0:T(512)S(1)}, u32[]{:S(2)}) copy-start(f32[384]{0:T(512)S(1)} %get-tuple-element.77) | copy-start | bytes 4612
  175.0 281.4 %copy-start.54 = (f32[384]{0:T(512)}, f32[384]{0:T(512)S(1)}, u32[]{:S(2)}) copy-start(f32[384]{0:T(512)S(1)} %get-tuple-element.74) | copy-start | bytes 4612
  339.6 124.3 %all-gather.10.cloned.1.call-start = ((), (), s32[]{:S(2)}) async-start(), calls=%async_computation | async-start | bytes 2396160 | tf_op jit(solution)/shard_map/all_gather | solution.py:53
  340.2 215.7 %all-gather.12.cloned.1.call-start = ((), (), s32[]{:S(2)}) async-start(), calls=%async_computation.1 | async-start | bytes 2396160 | tf_op jit(solution)/shard_map/all_gather | solution.py:54
  340.8 350.2 %all-reduce.27.cloned.1.call-start = ((), (), s32[]{:S(2)}) async-start(), calls=%async_computation.3 | async-start | bytes 1228800 | tf_op jit(solution)/shard_map/psum | solution.py:184
  655.1 258.3 %all-reduce.31.cloned.1.call-start = ((), (), s32[]{:S(2)}) async-start(), calls=%async_computation.5 | async-start | bytes 1228800 | tf_op jit(solution)/shard_map/psum | solution.py:113
  701.4 621.5 %all-reduce.25.cloned.1.call-start = ((), (), s32[]{:S(2)}) async-start(), calls=%async_computation.2 | async-start | bytes 21233664
  867.1 6.5 collective-permute-start.15
  868.4 8.4 collective-permute-start.14
  869.7 16.6 %collective-permute-start.13 = (f32[192,8]{0,1:T(8,128)S(1)}, f32[192,8]{0,1:T(8,128)S(1)}, u32[]{:S(2)}, u32[]{:S(2)}) collective-permute-start(f32[192,8]{0,1:T(8,128)S(1)} %fusion), channel_id=1, source_target_pairs={{0,28},{2,30},{4,32},{6,34},{8,36},{10,38},{12,40},{14,42},{16,44}... | collective-permute-start | bytes 18440
  871.0 17.5 %collective-permute-start.12 = (f32[192,8]{0,1:T(8,128)S(1)}, f32[192,8]{0,1:T(8,128)S(1)}, u32[]{:S(2)}, u32[]{:S(2)}) collective-permute-start(f32[192,8]{0,1:T(8,128)S(1)} %fusion), channel_id=1, source_target_pairs={{0,26},{2,28},{4,30},{6,32},{8,34},{10,36},{12,38},{14,40},{16,42}... | collective-permute-start | bytes 18440
  872.3 18.7 %collective-permute-start.11 = (f32[192,8]{0,1:T(8,128)S(1)}, f32[192,8]{0,1:T(8,128)S(1)}, u32[]{:S(2)}, u32[]{:S(2)}) collective-permute-start(f32[192,8]{0,1:T(8,128)S(1)} %fusion), channel_id=1, source_target_pairs={{0,24},{2,26},{4,28},{6,30},{8,32},{10,34},{12,36},{14,38},{16,40}... | collective-permute-start | bytes 18440
  873.6 21.2 %collective-permute-start.10 = (f32[192,8]{0,1:T(8,128)S(1)}, f32[192,8]{0,1:T(8,128)S(1)}, u32[]{:S(2)}, u32[]{:S(2)}) collective-permute-start(f32[192,8]{0,1:T(8,128)S(1)} %fusion), channel_id=1, source_target_pairs={{0,22},{2,24},{4,26},{6,28},{8,30},{10,32},{12,34},{14,36},{16,38}... | collective-permute-start | bytes 18440
  876.8 20.0 %collective-permute-start.9 = (f32[192,8]{0,1:T(8,128)S(1)}, f32[192,8]{0,1:T(8,128)S(1)}, u32[]{:S(2)}, u32[]{:S(2)}) collective-permute-start(f32[192,8]{0,1:T(8,128)S(1)} %fusion), channel_id=1, source_target_pairs={{0,20},{2,22},{4,24},{6,26},{8,28},{10,30},{12,32},{14,34},{16,36}... | collective-permute-start | bytes 18440
  886.4 13.1 collective-permute-start.8
  888.5 15.2 %collective-permute-start.7 = (f32[192,8]{0,1:T(8,128)S(1)}, f32[192,8]{0,1:T(8,128)S(1)}, u32[]{:S(2)}, u32[]{:S(2)}) collective-permute-start(f32[192,8]{0,1:T(8,128)S(1)} %fusion), channel_id=1, source_target_pairs={{0,16},{2,18},{4,20},{6,22},{8,24},{10,26},{12,28},{14,30},{16,32}... | collective-permute-start | bytes 18440
  891.0 14.3 %collective-permute-start.6 = (f32[192,8]{0,1:T(8,128)S(1)}, f32[192,8]{0,1:T(8,128)S(1)}, u32[]{:S(2)}, u32[]{:S(2)}) collective-permute-start(f32[192,8]{0,1:T(8,128)S(1)} %fusion), channel_id=1, source_target_pairs={{0,14},{2,16},{4,18},{6,20},{8,22},{10,24},{12,26},{14,28},{16,30}... | collective-permute-start | bytes 18440
  894.8 13.0 collective-permute-start.5
  896.9 14.1 %collective-permute-start.4 = (f32[192,8]{0,1:T(8,128)S(1)}, f32[192,8]{0,1:T(8,128)S(1)}, u32[]{:S(2)}, u32[]{:S(2)}) collective-permute-start(f32[192,8]{0,1:T(8,128)S(1)} %fusion), channel_id=1, source_target_pairs={{0,10},{2,12},{4,14},{6,16},{8,18},{10,20},{12,22},{14,24},{16,26}... | collective-permute-start | bytes 18440
  899.4 11.6 collective-permute-start.3
  903.7 7.3 collective-permute-start.2
  905.3 5.7 collective-permute-start.1
  907.8 3.5 collective-permute-start
  (104 other events, 3460.3 us)
Sparse Core Ops, SparseCore 0:
  339.7 36.0 all-reduce.28
  655.2 35.7 all-reduce.26
  701.5 38.7 all-reduce.30
  742.9 579.9 all-reduce.24
Sparse Core Ops, SparseCore 1:
  341.8 108.7 all-gather.9
  452.2 103.6 all-gather.11
where the time goes:
time: 1340 us
  blocking collectives  833 us (62%)
  waiting for transfers between devices  243 us (18%)
  local copies, waits for them, and re-layouts  105 us (8%)
  matrix products  51.3 us (4%)
  starting transfers between devices  42.1 us (3%)
  other arithmetic  41.3 us (3%)
  between operations  19.2 us (1%)
    unnamed x2, blocking collectives  421 us
    unnamed x23, waiting for transfers between devices  128 us
    all_gather x1, waiting for transfers between devices, fetch_layer(): lax.all_gather(w_out[layer_index], 'dp', axis=2, tiled=True)  85.3 us
    all_gather x1, blocking collectives, fetch_layer(): lax.all_gather(ln_bias[layer_index], 'dp', axis=1, tiled=True)  83.9 us
    all_gather x1, blocking collectives, fetch_layer(): lax.all_gather(w_proj[layer_index], 'dp', axis=1, tiled=True)  78.9 us
    all_gather x1, blocking collectives, fetch_layer(): lax.all_gather(w_qkv[layer_index], 'dp', axis=0, tiled=True)  78.6 us
    all_gather x1, blocking collectives, fetch_layer(): lax.all_gather(w_router[layer_index], 'dp', axis=0, tiled=True)  78.4 us
    all_gather x1, blocking collectives, fetch_layer(): lax.all_gather(ln_gain[layer_index], 'dp', axis=1, tiled=True)  77 us
  transfers between devices with their start and end apart: 22, of which 4 were waited for; matrix products, arithmetic and copies ran while one was open for 17% of the time, Pallas kernels for 0%

commit v1 on v0

--- a/solution.py
+++ b/solution.py
@@ -13,6 +13,11 @@
 EPSILON = 1e-06
 
 
+def all_by_exchange(shard, name, d):
+    outgoing = jnp.stack([shard] * lax.axis_size(name))
+    return jnp.concatenate(lax.all_to_all(outgoing, name, 0, 0), axis=d)
+
+
 def norm_forward(field, gain_row, shift_row):
     mean_value = jnp.mean(field, axis=-1, keepdims=True)
     centered = field - mean_value
@@ -48,7 +53,7 @@
 
 def fetch_layer(layer_index, w_qkv, w_proj, w_in, w_out, w_router, ln_gain, ln_bias):
     return (
-        lax.all_gather(w_qkv[layer_index], "dp", axis=0, tiled=True),
+        all_by_exchange(w_qkv[layer_index], "dp", 0),
         lax.all_gather(w_proj[layer_index], "dp", axis=1, tiled=True),
         lax.all_gather(w_in[layer_index], "dp", axis=1, tiled=True),
         lax.all_gather(w_out[layer_index], "dp", axis=2, tiled=True),

time: 1340 us -> 1280 us (0.955)
  blocking collectives: 833 us -> 754 us
    all_gather x1 -> x0, blocking collectives: 78.6 us -> none  [fetch_layer(): lax.all_gather(w_qkv[layer_index], 'dp', axis=0, tiled=True)]
  transfers between devices with their start and end apart: 22 -> 23, of which waited for: 4 -> 4; matrix products, arithmetic and copies ran while one was open for 17% -> 18% of each run, Pallas kernels for 0% -> 0%
where the time goes in v1:
time: 1280 us; the launch traced here: 1270 us
  blocking collectives  754 us (59%)
  waiting for transfers between devices  244 us (19%)
  local copies, waits for them, and re-layouts  104 us (8%)
  starting transfers between devices  51.9 us (4%)
  matrix products  51.3 us (4%)
  other arithmetic  41.3 us (3%)
  between operations  19.2 us (2%)
    unnamed x2, blocking collectives  422 us
    unnamed x23, waiting for transfers between devices  128 us
    all_gather x1, waiting for transfers between devices, fetch_layer(): lax.all_gather(w_out[layer_index], 'dp', axis=2, tiled=True)  86.3 us
    all_gather x1, blocking collectives, fetch_layer(): lax.all_gather(ln_bias[layer_index], 'dp', axis=1, tiled=True)  84.1 us
    all_gather x1, blocking collectives, fetch_layer(): lax.all_gather(w_proj[layer_index], 'dp', axis=1, tiled=True)  78.1 us
    all_gather x1, blocking collectives, fetch_layer(): lax.all_gather(w_router[layer_index], 'dp', axis=0, tiled=True)  77.8 us
    all_gather x1, blocking collectives, fetch_layer(): lax.all_gather(ln_gain[layer_index], 'dp', axis=1, tiled=True)  77.7 us
    unnamed x17, starting transfers between devices  41.6 us
  transfers between devices with their start and end apart: 23, of which 4 were waited for; matrix products, arithmetic and copies ran while one was open for 18% of the time, Pallas kernels for 0%

profile of v1, /device:TPU:0, one launch (start us, length us, event | category | flops | bytes accessed | tf_op | source)
XLA Modules:
  0.0 1265.8 jit_solution(18301074325375952698)
XLA Ops:
  9.7 9.9 all-to-all-start
  19.9 84.1 %all-gather.1 = bf16[1,2,384]{1,0,2:T(2,128)(2,1)S(1)} all-gather(bf16[1,2,6]{1,0,2:T(2,128)(2,1)S(1)} %copy.165), channel_id=3, replica_groups=mesh['dp'=64,'mp'=2] {'dp'}, dimensions={2}, use_global_device_ids=true | all-gather | bytes 1560 | tf_op jit(solution)/shard_map/all_gather | solution.py:62
  105.9 77.7 %all-gather = bf16[1,2,384]{1,0,2:T(2,128)(2,1)S(1)} all-gather(bf16[1,2,6]{1,0,2:T(2,128)(2,1)S(1)} %copy.164), channel_id=2, replica_groups=mesh['dp'=64,'mp'=2] {'dp'}, dimensions={2}, use_global_device_ids=true | all-gather | bytes 1560 | tf_op jit(solution)/shard_map/all_gather | solution.py:61
  185.6 78.1 %all-gather.2 = bf16[1,192,384]{1,0,2:T(2,128)(2,1)S(1)} all-gather(bf16[1,192,6]{1,0,2:T(2,128)(2,1)S(1)} %copy.170), channel_id=4, replica_groups=mesh['dp'=64,'mp'=2] {'dp'}, dimensions={2}, use_global_device_ids=true | all-gather | bytes 149760 | tf_op jit(solution)/shard_map/all_gather | solution.py:57
  274.8 5.9 gather_fusion.3
  284.4 5.9 gather_fusion
  298.7 77.8 %all-gather.3 = bf16[1,384,4]{2,0,1:T(2,128)(2,1)S(1)} all-gather(bf16[1,6,4]{2,0,1:T(2,128)(2,1)S(1)} %copy.174), channel_id=5, replica_groups=mesh['dp'=64,'mp'=2] {'dp'}, dimensions={1}, use_global_device_ids=true | all-gather | bytes 3120 | tf_op jit(solution)/shard_map/all_gather | solution.py:60
  400.3 86.3 %all-gather.11.cloned.1.call-done = bf16[1,4,768,384]{2,1,0,3:T(4,128)(2,1)} async-done(((bf16[1,4,768,6]{2,1,0,3:T(4,128)(2,1)}), bf16[1,4,768,384]{2,1,0,3:T(4,128)(2,1)}) %all-gather.11.cloned.1.call-update) | async-done | bytes 2359312 | tf_op jit(solution)/shard_map/all_gather | solution.py:59
  486.6 5.4 copy.182
  511.7 15.0 %all-reduce.16 = (f32[197,2]{1,0:T(8,128)}, f32[197,2]{1,0:T(8,128)}) all-reduce(f32[197,2]{1,0:T(8,128)} %reduce_sum.430, f32[197,2]{1,0:T(8,128)S(1)} %reduce_sum.420), channel_id=1, replica_groups=mesh['dp'=64,'mp'=2] {'mp'}, use_global_device_ids=true, to_apply=%region_49.54 | all-reduce | flops 788 | bytes 6304 | tf_op jit(solution)/shard_map/psum | solution.py:189
  530.5 3.6 scatter_custom_fusion.2
  535.0 4.1 fusion.30
  555.7 4.1 fusion.27
  563.6 4.1 fusion.199
  586.1 5.7 convolution_add_fusion.1
  591.8 30.0 %all-reduce.27.cloned.1.call-done = (f32[197,384]{1,0:T(8,128)}, f32[197,384]{1,0:T(8,128)}) async-done(((f32[197,384]{1,0:T(8,128)}, f32[197,384]{1,0:T(8,128)}), (f32[197,384]{1,0:T(8,128)}, f32[197,384]{1,0:T(8,128)})) %all-reduce.27.cloned.1.call-update) | async-done | bytes 605200 | tf_op jit(solution)/shard_map/psum | solution.py:189
  635.7 7.5 copy.205
  643.2 5.2 copy.206
  652.2 145.4 %fusion = f32[192,8]{0,1:T(8,128)S(1)} fusion(f32[192,384]{0,1:T(8,128)S(1)} %convolution_add_fusion.3), kind=kCustom, calls=%all-reduce-scatter | all-reduce-scatter fusion | flops 98305 | bytes 301568
  807.3 9.5 collective-permute-start.9
  821.4 3.8 collective-permute-start.6
  829.9 4.3 collective-permute-start.3
  849.1 276.1 %all-reduce.14 = (f32[384,4]{0,1:T(4,128)S(1)}, f32[2,384]{1,0:T(2,128)S(1)}, f32[2,384]{1,0:T(2,128)S(1)}) all-reduce(f32[384,4]{0,1:T(4,128)S(1)} %convolution_add_fusion.6, f32[2,384]{1,0:T(2,128)S(1)} %maximum_add_fusion, f32[2,384]{1,0:T(2,128)S(1)} %maximum_add_fusion.1), channel_id=12, replica_groups=mesh['dp'=64,'mp'=2] {'dp'}, use_global_device_ids=true, to_apply=%region_62.67.clone | all-reduce | flops 3072 | bytes 24576
  1127.2 126.6 %all-reduce.25.cloned.1.call-done = (f32[384,3,192]{2,0,1:T(8,128)}, f32[4,384,768]{2,0,1:T(4,128)}, f32[4,768,384]{1,0,2:T(4,128)}) async-done(((f32[384,3,192]{2,0,1:T(8,128)}, f32[4,384,768]{2,0,1:T(4,128)}, f32[4,768,384]{1,0,2:T(4,128)}), (f32[384,3,192]{2,0,1:T(8,128)}, f32[4,384,768]{2,0,1:T(4,128)}, f32[4,768,384]{1,0,2:T(4,128)})) %all-reduce.25.cloned.1.call-update) | async-done | bytes 10321936
  (485 shorter events, 170.6 us)
Async XLA Ops:
  9.7 255.9 %all-to-all-start = ((bf16[64,6,3,192]{3,1,2,0:T(8,128)(2,1)}), bf16[64,6,3,192]{3,1,2,0:T(8,128)(2,1)S(1)}, u32[]{:S(2)}, u32[]{:S(2)}) async-start(bf16[64,6,3,192]{3,1,2,0:T(8,128)(2,1)} %stack.87), calls=%async_computation | async-start | bytes 1572864 | tf_op jit(solution)/shard_map/all_to_all | solution.py:18
  19.6 365.0 %all-reduce.29.cloned.1.call-start = ((), (), s32[]{:S(2)}) async-start(), calls=%async_computation.5 | async-start | bytes 1228800 | tf_op jit(solution)/shard_map/psum | solution.py:95
  185.6 200.7 %copy-start.50 = (f32[384]{0:T(512)}, f32[384]{0:T(512)S(1)}, u32[]{:S(2)}) copy-start(f32[384]{0:T(512)S(1)} %get-tuple-element.74) | copy-start | bytes 4612
  270.7 122.9 %all-gather.9.cloned.1.call-start = ((), (), s32[]{:S(2)}) async-start(), calls=%async_computation.1 | async-start | bytes 2396160 | tf_op jit(solution)/shard_map/all_gather | solution.py:58
  271.3 215.3 %all-gather.11.cloned.1.call-start = ((), (), s32[]{:S(2)}) async-start(), calls=%async_computation.2 | async-start | bytes 2396160 | tf_op jit(solution)/shard_map/all_gather | solution.py:59
  271.9 349.9 %all-reduce.27.cloned.1.call-start = ((), (), s32[]{:S(2)}) async-start(), calls=%async_computation.4 | async-start | bytes 1228800 | tf_op jit(solution)/shard_map/psum | solution.py:189
  585.8 258.0 %all-reduce.31.cloned.1.call-start = ((), (), s32[]{:S(2)}) async-start(), calls=%async_computation.6 | async-start | bytes 1228800 | tf_op jit(solution)/shard_map/psum | solution.py:118
  632.2 621.5 %all-reduce.25.cloned.1.call-start = ((), (), s32[]{:S(2)}) async-start(), calls=%async_computation.3 | async-start | bytes 21233664
  797.6 6.5 collective-permute-start.15
  798.9 8.4 collective-permute-start.14
  800.2 16.6 %collective-permute-start.13 = (f32[192,8]{0,1:T(8,128)S(1)}, f32[192,8]{0,1:T(8,128)S(1)}, u32[]{:S(2)}, u32[]{:S(2)}) collective-permute-start(f32[192,8]{0,1:T(8,128)S(1)} %fusion), channel_id=1, source_target_pairs={{0,28},{2,30},{4,32},{6,34},{8,36},{10,38},{12,40},{14,42},{16,44}... | collective-permute-start | bytes 18440
  801.5 17.5 %collective-permute-start.12 = (f32[192,8]{0,1:T(8,128)S(1)}, f32[192,8]{0,1:T(8,128)S(1)}, u32[]{:S(2)}, u32[]{:S(2)}) collective-permute-start(f32[192,8]{0,1:T(8,128)S(1)} %fusion), channel_id=1, source_target_pairs={{0,26},{2,28},{4,30},{6,32},{8,34},{10,36},{12,38},{14,40},{16,42}... | collective-permute-start | bytes 18440
  802.8 18.7 %collective-permute-start.11 = (f32[192,8]{0,1:T(8,128)S(1)}, f32[192,8]{0,1:T(8,128)S(1)}, u32[]{:S(2)}, u32[]{:S(2)}) collective-permute-start(f32[192,8]{0,1:T(8,128)S(1)} %fusion), channel_id=1, source_target_pairs={{0,24},{2,26},{4,28},{6,30},{8,32},{10,34},{12,36},{14,38},{16,40}... | collective-permute-start | bytes 18440
  804.1 21.2 %collective-permute-start.10 = (f32[192,8]{0,1:T(8,128)S(1)}, f32[192,8]{0,1:T(8,128)S(1)}, u32[]{:S(2)}, u32[]{:S(2)}) collective-permute-start(f32[192,8]{0,1:T(8,128)S(1)} %fusion), channel_id=1, source_target_pairs={{0,22},{2,24},{4,26},{6,28},{8,30},{10,32},{12,34},{14,36},{16,38}... | collective-permute-start | bytes 18440
  807.3 20.0 %collective-permute-start.9 = (f32[192,8]{0,1:T(8,128)S(1)}, f32[192,8]{0,1:T(8,128)S(1)}, u32[]{:S(2)}, u32[]{:S(2)}) collective-permute-start(f32[192,8]{0,1:T(8,128)S(1)} %fusion), channel_id=1, source_target_pairs={{0,20},{2,22},{4,24},{6,26},{8,28},{10,30},{12,32},{14,34},{16,36}... | collective-permute-start | bytes 18440
  816.8 13.1 %collective-permute-start.8 = (f32[192,8]{0,1:T(8,128)S(1)}, f32[192,8]{0,1:T(8,128)S(1)}, u32[]{:S(2)}, u32[]{:S(2)}) collective-permute-start(f32[192,8]{0,1:T(8,128)S(1)} %fusion), channel_id=1, source_target_pairs={{0,18},{2,20},{4,22},{6,24},{8,26},{10,28},{12,30},{14,32},{16,34}... | collective-permute-start | bytes 18440
  819.0 15.2 %collective-permute-start.7 = (f32[192,8]{0,1:T(8,128)S(1)}, f32[192,8]{0,1:T(8,128)S(1)}, u32[]{:S(2)}, u32[]{:S(2)}) collective-permute-start(f32[192,8]{0,1:T(8,128)S(1)} %fusion), channel_id=1, source_target_pairs={{0,16},{2,18},{4,20},{6,22},{8,24},{10,26},{12,28},{14,30},{16,32}... | collective-permute-start | bytes 18440
  821.4 14.3 %collective-permute-start.6 = (f32[192,8]{0,1:T(8,128)S(1)}, f32[192,8]{0,1:T(8,128)S(1)}, u32[]{:S(2)}, u32[]{:S(2)}) collective-permute-start(f32[192,8]{0,1:T(8,128)S(1)} %fusion), channel_id=1, source_target_pairs={{0,14},{2,16},{4,18},{6,20},{8,22},{10,24},{12,26},{14,28},{16,30}... | collective-permute-start | bytes 18440
  825.3 13.0 %collective-permute-start.5 = (f32[192,8]{0,1:T(8,128)S(1)}, f32[192,8]{0,1:T(8,128)S(1)}, u32[]{:S(2)}, u32[]{:S(2)}) collective-permute-start(f32[192,8]{0,1:T(8,128)S(1)} %fusion), channel_id=1, source_target_pairs={{0,12},{2,14},{4,16},{6,18},{8,20},{10,22},{12,24},{14,26},{16,28}... | collective-permute-start | bytes 18440
  827.3 14.1 %collective-permute-start.4 = (f32[192,8]{0,1:T(8,128)S(1)}, f32[192,8]{0,1:T(8,128)S(1)}, u32[]{:S(2)}, u32[]{:S(2)}) collective-permute-start(f32[192,8]{0,1:T(8,128)S(1)} %fusion), channel_id=1, source_target_pairs={{0,10},{2,12},{4,14},{6,16},{8,18},{10,20},{12,22},{14,24},{16,26}... | collective-permute-start | bytes 18440
  829.9 11.6 collective-permute-start.3
  834.2 7.3 collective-permute-start.2
  835.8 5.7 collective-permute-start.1
  838.3 3.5 collective-permute-start
  (103 other events, 3405.7 us)
Sparse Core Ops, SparseCore 0:
  270.8 35.4 all-reduce.28
  585.9 35.7 all-reduce.26
  632.3 38.7 all-reduce.30
  673.8 579.9 all-reduce.24
Sparse Core Ops, SparseCore 1:
  272.9 108.1 all-gather.8
  382.6 103.9 all-gather.10
